TPU v7x, 32 devices: a whole 2x2x4 slice. The times are simulated.
32 devices in a mesh: groups: 2 (over y), hx: 16 (over z, x, core).
Axes of the slice: x: 2, y: 2, z: 4, core: 2. Of those that a mesh axis runs over, the one named last changes fastest.
Arguments:
- tokens: bfloat16 [32, 8192], P(('groups', 'hx')), parts along dimension 0, may hold values from -6 to 6
- gate_codes: bfloat16 [8192, 26624], P(None, 'hx'), may hold values from -8 to 7, as said below
- gate_scales: float32 [64, 26624], P(None, 'hx'), may hold values from 0.00077339803 to 0.00773398
- up_codes: bfloat16 [8192, 26624], P(None, 'hx'), may hold values from -8 to 7, as said below
- up_scales: float32 [64, 26624], P(None, 'hx'), may hold values from 0.00077339803 to 0.00773398
- down_codes: bfloat16 [26624, 8192], P('hx'), may hold values from -8 to 7, as said below
- down_scales: float32 [8192], replicated, may hold values from 0.00061286293 to 0.006128629
- hadamard: int32 [52, 52], replicated, may hold values from -1 to 1, as said below
Outputs:
- mixed: bfloat16 [32, 8192], P(('groups', 'hx')), parts along dimension 0
There are 2 independent parts, one for each index of `groups`. A program takes and returns all parts, laid end to end along the dimension named above; an argument that names none is the same for every part. Nothing has to cross between parts.
Inputs may be any that keep to these rules, and one draw needn't show every extreme that they name: `gate_codes`: whole numbers. `up_codes`: whole numbers. `down_codes`: whole numbers. `hadamard`: a Hadamard matrix: every entry is -1 or 1 and any two rows are orthogonal.
All inputs are finite; a program needn't handle non-finite values.
Results may differ from a plain program's by a relative error of at most 0.015.
Values may be sent and summed in bfloat16 or wider, within the bound.
A program may use at most 192 MiB of HBM per device.

v0:
```python
import math

import jax
import jax.numpy as jnp
from jax import lax
from jax.sharding import PartitionSpec as P

HA = 512
HB = 52
FF = 26624


def sylvester(size):
    index_vec = jnp.arange(size, dtype=jnp.int32)
    parity = jnp.zeros((size, size), jnp.int32)
    for level in range(max(size.bit_length() - 1, 0)):
        left_bits = jnp.right_shift(index_vec[:, None], level) & 1
        right_bits = jnp.right_shift(index_vec[None, :], level) & 1
        parity = parity + left_bits * right_bits
    return (1 - 2 * (parity % 2)).astype(jnp.float32)


def dequantize(codes, scales):
    row_total, col_total = codes.shape
    group_total = scales.shape[0]
    grouped = codes.astype(jnp.float32).reshape(group_total, row_total // group_total, col_total)
    return (grouped * scales[:, None, :]).reshape(row_total, col_total).astype(jnp.bfloat16)


def per_device(
    tokens, gate_codes, gate_scales, up_codes, up_scales, down_codes, down_scales, hadamard
):
    gate_weight = dequantize(gate_codes, gate_scales)
    up_weight = dequantize(up_codes, up_scales)
    tile_rows = lax.all_gather(tokens, "hx", axis=0, tiled=True)
    gate = jnp.dot(tile_rows, gate_weight, preferred_element_type=jnp.float32)
    up_part = jnp.dot(tile_rows, up_weight, preferred_element_type=jnp.float32)
    hidden = jax.nn.silu(gate) * up_part
    factor = hadamard.astype(jnp.float32)
    gathered = lax.all_to_all(
        hidden.astype(jnp.bfloat16), "hx", split_axis=0, concat_axis=1, tiled=True
    ).astype(hidden.dtype)
    row_count = gathered.shape[0]
    cube = gathered.reshape(row_count, HA, HB)
    cube = jnp.einsum("tab,ac->tcb", cube, sylvester(HA), precision=lax.Precision.HIGHEST)
    cube = jnp.einsum("tcb,bd->tcd", cube, factor, precision=lax.Precision.HIGHEST)
    turned = lax.all_to_all(
        cube.reshape(row_count, FF).astype(jnp.bfloat16),
        "hx",
        split_axis=1,
        concat_axis=0,
        tiled=True,
    ).astype(jnp.float32)
    rotated = (turned * (1.0 / math.sqrt(FF))).astype(jnp.bfloat16)
    summed = lax.psum_scatter(
        jnp.dot(rotated, down_codes, preferred_element_type=jnp.float32),
        "hx",
        scatter_dimension=0,
        tiled=True,
    )
    mixed = (summed * down_scales[None, :]).astype(jnp.bfloat16)
    return mixed


def solution(mesh):
    in_specs = (
        P(("groups", "hx"), None),
        P(None, "hx"),
        P(None, "hx"),
        P(None, "hx"),
        P(None, "hx"),
        P("hx", None),
        P(),
        P(),
    )
    out_specs = P(("groups", "hx"), None)
    return jax.shard_map(
        per_device, mesh=mesh, in_specs=in_specs, out_specs=out_specs, check_vma=False
    )
```

profile of v0, /device:TPU:0, one launch (start us, length us, event | category | flops | bytes accessed | tf_op | source)
XLA Modules:
  0.0 227.9 jit_solution(11263058405985309339)
XLA Ops:
  6.5 24.8 %all-gather = bf16[16,1,8192]{2,1,0:T(2,128)(2,1)S(1)} all-gather(bf16[1,1,8192]{2,1,0:T(2,128)(2,1)} %bitcast.40), channel_id=1, replica_groups=mesh['groups'=2,'hx'=16] {'hx'}, dimensions={0}, use_global_device_ids=true | all-gather | bytes 278528 | tf_op jit(solution)/shard_map/all_gather | solution.py:35
  31.3 19.3 %fusion.1 = bf16[8192,1664]{1,0:T(8,128)(2,1)} fusion(bf16[8192,1664]{1,0:T(8,128)(2,1)} %param.9, f32[64,1664]{1,0:T(8,128)} %param.10), kind=kLoop, calls=%fused_computation.3 | loop fusion | flops 40894464 | bytes 54951936 | tf_op jit(solution)/shard_map/convert_element_type | solution.py:27
  50.7 0.0 copy-start
  50.7 10.7 %convolution_bitcast_fusion.1 = f32[16,1664]{1,0:T(8,128)S(1)} fusion(bf16[8192,1664]{1,0:T(8,128)(2,1)} %fusion.1, bf16[16,1,8192]{2,1,0:T(2,128)(2,1)S(1)} %all-gather), kind=kOutput, calls=%fused_computation.6 | convolution fusion | flops 436207616 | bytes 27631616 | tf_op jit(solution)/shard_map/dot_general | solution.py:36
  61.4 0.0 copy-done
  61.5 19.2 %fusion = bf16[8192,1664]{1,0:T(8,128)(2,1)} fusion(bf16[8192,1664]{1,0:T(8,128)(2,1)} %param.11, f32[64,1664]{1,0:T(8,128)S(1)} %copy-done), kind=kLoop, calls=%fused_computation.1 | loop fusion | flops 40894464 | bytes 54951936 | tf_op jit(solution)/shard_map/convert_element_type | solution.py:27
  80.6 10.7 %fusion.4 = bf16[16,1,1664]{2,0,1:T(8,128)(2,1)S(1)} fusion(bf16[8192,1664]{1,0:T(8,128)(2,1)} %fusion, f32[16,1664]{1,0:T(8,128)S(1)} %convolution_bitcast_fusion.1, bf16[16,1,8192]{2,1,0:T(2,128)(2,1)S(1)} %all-gather), kind=kOutput, calls=%fused_computation.8 | convolution fusion | flops 436367360 | bytes 27684864 | tf_op jit(solution)/shard_map/dot_general | solution.py:37
  91.4 0.0 copy-start.3
  91.4 0.0 copy-start.1
  91.4 0.5 broadcast.214
  91.9 0.7 reduce.1
  92.6 0.7 reshape.182
  93.3 3.5 %all-to-all-start = ((bf16[16,2,832]{2,1,0:T(2,128)(2,1)}), bf16[16,2,832]{2,1,0:T(2,128)(2,1)S(1)}, u32[]{:S(2)}, u32[]{:S(2)}) async-start(bf16[16,2,832]{2,1,0:T(2,128)(2,1)} %reshape.182), calls=%async_computation | async-start | bytes 114688 | tf_op jit(solution)/shard_map/all_to_all | solution.py:40
  96.8 0.0 all-reduce.3.cloned.1.call-start
  96.9 6.7 %all-to-all-done = bf16[16,2,832]{2,1,0:T(2,128)(2,1)S(1)} async-done(((bf16[16,2,832]{2,1,0:T(2,128)(2,1)}), bf16[16,2,832]{2,1,0:T(2,128)(2,1)S(1)}, u32[]{:S(2)}, u32[]{:S(2)}) %all-to-all-start) | async-done | bytes 53280 | tf_op jit(solution)/shard_map/all_to_all | solution.py:40
  103.6 0.1 reshape.183
  103.7 0.3 reduce
  104.0 0.4 reshape.177
  104.4 1.7 fusion.9
  106.2 0.0 copy-done.2
  106.2 0.3 convolution_convert_fusion
  106.5 0.1 copy.14
  106.6 0.2 convert_element_type.63
  106.9 0.9 reduce.2
  107.8 0.1 reshape.184
  107.9 9.4 %all_to_all.23 = bf16[16,2,832]{2,1,0:T(2,128)(2,1)S(1)} all-to-all(bf16[16,2,832]{2,1,0:T(2,128)(2,1)S(1)} %reshape.184), channel_id=1, replica_groups=mesh['groups'=2,'hx'=16] {'hx'}, dimensions={0} | all-to-all | bytes 106496 | tf_op jit(solution)/shard_map/all_to_all | solution.py:47
  117.3 0.1 reshape.185
  117.5 13.2 %fusion.40 = f32[16,8192]{1,0:T(8,128)} fusion(bf16[1664,8192]{1,0:T(8,128)(2,1)} %param.13, bf16[1,16,1664]{2,0,1:T(2,128)(2,1)S(1)} %bitcast.39), kind=kOutput, calls=%fused_computation.48 | convolution fusion | flops 436287488 | bytes 27840512 | tf_op jit(solution)/shard_map/dot_general | solution.py:56
  130.7 0.0 all-reduce.3.cloned.1.call-update
  130.7 0.6 dynamic-slice
  131.3 87.5 %all-reduce.3.cloned.1.call-done = f32[16,8192]{1,0:T(8,128)} async-done(((f32[16,8192]{1,0:T(8,128)}), f32[16,8192]{1,0:T(8,128)}) %all-reduce.3.cloned.1.call-update) | async-done | bytes 524304
  218.8 2.2 fusion.44
  (8 shorter events, 0.0 us)
Async XLA Ops:
  50.7 10.8 %copy-start = (f32[64,1664]{1,0:T(8,128)S(1)}, f32[64,1664]{1,0:T(8,128)}, u32[]{:S(2)}) copy-start(f32[64,1664]{1,0:T(8,128)} %param.12) | copy-start | bytes 1277956
  80.6 25.5 %copy-start.2 = (s32[52,52]{1,0:T(8,128)S(1)}, s32[52,52]{1,0:T(8,128)}, u32[]{:S(2)}) copy-start(s32[52,52]{1,0:T(8,128)} %param.15) | copy-start | bytes 32452
  91.4 39.3 %copy-start.3 = (u32[32]{0:T(128)S(1)}, u32[32]{0:T(128)}, u32[]{:S(2)}) copy-start(u32[32]{0:T(128)} %constant.24) | copy-start | bytes 388
  91.4 127.4 %copy-start.1 = (f32[8192]{0:T(1024)S(1)}, f32[8192]{0:T(1024)}, u32[]{:S(2)}) copy-start(f32[8192]{0:T(1024)} %param.14) | copy-start | bytes 98308
  93.3 10.3 %all-to-all-start = ((bf16[16,2,832]{2,1,0:T(2,128)(2,1)}), bf16[16,2,832]{2,1,0:T(2,128)(2,1)S(1)}, u32[]{:S(2)}, u32[]{:S(2)}) async-start(bf16[16,2,832]{2,1,0:T(2,128)(2,1)} %reshape.182), calls=%async_computation | async-start | bytes 114688 | tf_op jit(solution)/shard_map/all_to_all | solution.py:40
  96.8 122.0 %all-reduce.3.cloned.1.call-start = ((), (), s32[]{:S(2)}) async-start(), calls=%async_computation.2 | async-start | bytes 1048576
Sparse Core Ops, SparseCore 0:
  130.8 87.9 all-reduce.2
where the time goes:
time: 228 us
  waiting for transfers between devices  94.2 us (41%)
  other arithmetic  42.7 us (19%)
  matrix products  36.7 us (16%)
  blocking collectives  34.2 us (15%)
  between operations  13.6 us (6%)
  starting transfers between devices  3.52 us (2%)
  local copies, waits for them, and re-layouts  3.02 us (1%)
    unnamed x2, waiting for transfers between devices  87.5 us
    convert_element_type x2, other arithmetic, dequantize(): (grouped * scales[:, None, :]).reshape(row_total, col_total)  38.5 us
    all_gather x1, blocking collectives, per_device(): tile_rows = lax.all_gather(tokens, 'hx', axis=0, tiled=True)  24.8 us
    dot_general x1, matrix products, per_device(): jnp.dot(rotated, down_codes, preferred_element_type=jnp.float32)  13.2 us
    dot_general x1, matrix products, per_device(): gate = jnp.dot(tile_rows, gate_weight, preferred_element_type=jnp.float32)  10.7 us
    dot_general x1, matrix products, per_device(): up_part = jnp.dot(tile_rows, up_weight, preferred_element_type=jnp.float32)  10.7 us
    all_to_all x1, blocking collectives, per_device(): lax.all_to_all(cube.reshape(row_count, FF).astype(jnp.bfloat16), 'hx', sp...  9.4 us
    all_to_all x1, waiting for transfers between devices, per_device(): lax.all_to_all(hidden.astype(jnp.bfloat16), 'hx', split_axis=0, concat_ax...  6.69 us
  transfers between devices with their start and end apart: 2, of which 2 were waited for; matrix products, arithmetic and copies ran while one was open for 0% of the time, Pallas kernels for 0%

commit v1 on v0

--- a/solution.py
+++ b/solution.py
@@ -1,8 +1,11 @@
+import functools
 import math
 
 import jax
 import jax.numpy as jnp
 from jax import lax
+from jax.experimental import pallas as pl
+from jax.experimental.pallas import tpu as pltpu
 from jax.sharding import PartitionSpec as P
 
 HA = 512
@@ -27,9 +30,337 @@
     return (grouped * scales[:, None, :]).reshape(row_total, col_total).astype(jnp.bfloat16)
 
 
+LANES = 128
+ROWS = 16
+CHUNK_GROUPS = 4
+SLOTS = 7
+
+
+def kernel(
+    n, tok_ref, gate_ref, gscale_ref, up_ref, uscale_ref, down_ref, dscale_ref, spread_ref, table_ref,
+    out_ref,
+    ring, gs, us, down, ds, spread, table, local, tok, stage, lhs, acc, zbuf, recv_z, rbuf, rot, part, sendbuf, recv_c,
+    ring_sem, load_sem, down_sem, tok_own, tok_send, tok_recv, z_send, z_recv, r_send, r_recv, c_send, c_recv,
+):
+    me = lax.axis_index("hx")
+    pieces = tok.shape[0]
+    units = gate_ref.shape[1]
+    owners = units // LANES
+    chunk_rows = ring.shape[2]
+    chunks = gate_ref.shape[0] // chunk_rows
+    down_chunks, _, down_cols = down.shape
+    out_pieces = recv_c.shape[0]
+    peers = [lax.rem(me + step, n) for step in range(1, n)]
+
+    def gate_copy(c, slot):
+        rows = pl.ds(pl.multiple_of(c * chunk_rows, chunk_rows), chunk_rows)
+        return pltpu.make_async_copy(gate_ref.at[rows], ring.at[slot, 0], ring_sem.at[slot, 0])
+
+    def up_copy(c, slot):
+        rows = pl.ds(pl.multiple_of(c * chunk_rows, chunk_rows), chunk_rows)
+        return pltpu.make_async_copy(up_ref.at[rows], ring.at[slot, 1], ring_sem.at[slot, 1])
+
+    def down_copy(c):
+        cols = pl.ds(pl.multiple_of(c * down_cols, down_cols), down_cols)
+        return pltpu.make_async_copy(down_ref.at[:, cols], down.at[c], down_sem.at[c])
+
+    loads = [
+        pltpu.make_async_copy(src, dst, load_sem.at[i])
+        for i, (src, dst) in enumerate(
+            ((spread_ref, spread), (table_ref, table), (gscale_ref, gs), (uscale_ref, us), (dscale_ref, ds))
+        )
+    ]
+    own_tok = [
+        pltpu.make_async_copy(tok_ref.at[pl.ds(p * ROWS, ROWS)], tok.at[p, me], tok_own.at[p])
+        for p in range(pieces)
+    ]
+
+    barrier = pltpu.get_barrier_semaphore()
+    for peer in peers:
+        pl.semaphore_signal(barrier, inc=1, device_id={"hx": peer}, device_id_type=pl.DeviceIdType.MESH)
+    for copy in own_tok:
+        copy.start()
+    for copy in loads:
+        copy.start()
+    for c in range(SLOTS):
+        gate_copy(c, c).start()
+        up_copy(c, c).start()
+    pl.semaphore_wait(barrier, n - 1)
+
+    def remote(src, dst, send_sem, recv_sem, peer):
+        return pltpu.make_async_remote_copy(
+            src_ref=src, dst_ref=dst, send_sem=send_sem, recv_sem=recv_sem,
+            device_id={"hx": peer}, device_id_type=pl.DeviceIdType.MESH,
+        )
+
+    def tok_out(p, i):
+        return remote(
+            tok_ref.at[pl.ds(p * ROWS, ROWS)], tok.at[p, me], tok_send.at[p, i], tok_recv.at[p, me], peers[i]
+        )
+
+    def tok_in(p, i):
+        return remote(
+            tok_ref.at[pl.ds(p * ROWS, ROWS)], tok.at[p, peers[i]], tok_send.at[p, i], tok_recv.at[p, peers[i]],
+            peers[i],
+        )
+
+    for p in range(pieces):
+        for i in range(n - 1):
+            tok_out(p, i).start()
+
+    lhs[...] = jnp.zeros_like(lhs)
+    acc[...] = jnp.zeros_like(acc)
+    for copy in loads:
+        copy.wait()
+
+    def build(i, carry):
+        rows = pl.ds(pl.multiple_of(i * LANES, LANES), LANES)
+        both = jnp.dot(spread[rows, :], table[...], preferred_element_type=jnp.float32)
+        local[rows, :] = (both[:, :units] * both[:, units:]).astype(jnp.bfloat16)
+        return carry
+
+    lax.fori_loop(0, units // LANES, build, 0)
+
+    pairs_piece = ROWS // 2
+    chunks_piece = chunks // pieces
+    pairs_chunk = CHUNK_GROUPS // 2
+    for p in range(pieces):
+        own_tok[p].wait()
+        for i in range(n - 1):
+            tok_in(p, i).wait_recv()
+        stage[...] = tok[p].reshape(n * ROWS, LANES).astype(jnp.float32)
+        for q in range(pairs_piece):
+            lhs[q, :n, :LANES] = stage[pl.ds(2 * q, n, stride=ROWS), :].astype(jnp.bfloat16)
+            lhs[q, n:, LANES:] = stage[pl.ds(2 * q + 1, n, stride=ROWS), :].astype(jnp.bfloat16)
+
+        def step(k, carry):
+            c = p * chunks_piece + k
+            slot = lax.rem(c, SLOTS)
+            gate_copy(c, slot).wait()
+            up_copy(c, slot).wait()
+            for q in range(pairs_chunk):
+                left = lhs[k * pairs_chunk + q]
+                row = c * CHUNK_GROUPS + 2 * q
+                for w, scale in ((0, gs), (1, us)):
+                    res = jnp.dot(
+                        left, ring[slot, w, 2 * q * LANES : 2 * (q + 1) * LANES, :],
+                        preferred_element_type=jnp.float32,
+                    )
+                    acc[w] += res[:n] * scale[pl.ds(row, 1), :] + res[n:] * scale[pl.ds(row + 1, 1), :]
+
+            @pl.when(c + SLOTS < chunks)
+            def _():
+                gate_copy(c + SLOTS, slot).start()
+                up_copy(c + SLOTS, slot).start()
+
+            @pl.when(jnp.logical_and(c + SLOTS >= chunks, c + SLOTS - chunks < down_chunks))
+            def _():
+                down_copy(c + SLOTS - chunks).start()
+
+            return carry
+
+        lax.fori_loop(0, chunks_piece, step, 0)
+    for c in range(SLOTS, down_chunks):
+        down_copy(c).start()
+
+    gate = acc[0]
+    hidden = (gate / (1.0 + jnp.exp(-gate)) * acc[1]).astype(jnp.bfloat16)
+    turned = jnp.dot(hidden, local[...], preferred_element_type=jnp.float32).astype(jnp.bfloat16)
+    for j in range(owners):
+        zbuf[j] = turned[:, j * LANES : (j + 1) * LANES]
+
+    def z_out(j):
+        return remote(zbuf.at[j], recv_z.at[me], z_send.at[j], z_recv.at[me], j)
+
+    for j in range(owners):
+
+        @pl.when(me != j)
+        def _():
+            z_out(j).start()
+
+        @pl.when(me == j)
+        def _():
+            recv_z[j] = zbuf[j]
+
+    def r_out(i):
+        return remote(rbuf.at[peers[i]], rot.at[me], r_send.at[i], r_recv.at[me], peers[i])
+
+    @pl.when(me < owners)
+    def _():
+        for i in range(n - 1):
+            remote(zbuf.at[0], recv_z.at[peers[i]], z_send.at[0], z_recv.at[peers[i]], peers[i]).wait_recv()
+        cube = [recv_z[h].astype(jnp.float32) for h in range(n)]
+        span = 1
+        while span < n:
+            nxt = list(cube)
+            for h in range(n):
+                if h & span == 0:
+                    nxt[h] = cube[h] + cube[h | span]
+                    nxt[h | span] = cube[h] - cube[h | span]
+            cube = nxt
+            span *= 2
+        for h in range(n):
+            rbuf[h] = (cube[h] * (1.0 / math.sqrt(FF))).astype(jnp.bfloat16)
+        for i in range(n - 1):
+            r_out(i).start()
+        rot[me] = rbuf[me]
+
+    for j in range(owners):
+
+        @pl.when(me != j)
+        def _():
+            remote(rbuf.at[0], rot.at[j], r_send.at[0], r_recv.at[j], j).wait_recv()
+
+    rotated = jnp.concatenate([rot[j] for j in range(owners)], axis=1)
+
+    def c_out(p, i):
+        return remote(sendbuf.at[p, peers[i]], recv_c.at[p, me], c_send.at[p, i], c_recv.at[p, me], peers[i])
+
+    def c_in(p, i):
+        return remote(
+            sendbuf.at[p, peers[i]], recv_c.at[p, peers[i]], c_send.at[p, i], c_recv.at[p, peers[i]], peers[i]
+        )
+
+    per_piece = down_chunks // out_pieces
+    blocks = down_cols // LANES
+    for p in range(out_pieces):
+        for k in range(per_piece):
+            c = p * per_piece + k
+            down_copy(c).wait()
+            res = jnp.dot(rotated, down[c], preferred_element_type=jnp.float32)
+            for b in range(blocks):
+                part[pl.ds(k * blocks + b, n, stride=ROWS), :] = res[:, b * LANES : (b + 1) * LANES]
+        sendbuf[p] = part[...].astype(jnp.bfloat16).reshape(n, ROWS, LANES)
+        for i in range(n - 1):
+            c_out(p, i).start()
+        recv_c[p, me] = sendbuf[p, me]
+
+    for p in range(out_pieces):
+        for i in range(n - 1):
+            c_in(p, i).wait_recv()
+        total = recv_c[p, 0].astype(jnp.float32)
+        for h in range(1, n):
+            total = total + recv_c[p, h].astype(jnp.float32)
+        rows = slice(p * ROWS, (p + 1) * ROWS)
+        out_ref[rows, :] = (total * ds[rows, :]).astype(out_ref.dtype)
+
+    for p in range(pieces):
+        for i in range(n - 1):
+            tok_out(p, i).wait_send()
+    for j in range(owners):
+
+        @pl.when(me != j)
+        def _():
+            z_out(j).wait_send()
+
+    @pl.when(me < owners)
+    def _():
+        for i in range(n - 1):
+            r_out(i).wait_send()
+
+    for p in range(out_pieces):
+        for i in range(n - 1):
+            c_out(p, i).wait_send()
+
+
+def fused(n, tokens, gate_codes, gate_scales, up_codes, up_scales, down_codes, down_scales, hadamard):
+    depth, units = gate_codes.shape
+    width = down_codes.shape[1]
+    local_a = HA // n
+    unit = jnp.arange(units, dtype=jnp.int32)
+    lane = jnp.arange(LANES, dtype=jnp.int32)
+    half = LANES // 2
+    spread = (
+        (lane[None, :] == (unit % HB)[:, None]) | (lane[None, :] == half + (unit // HB)[:, None])
+    ).astype(jnp.bfloat16)
+    small = jnp.tile(hadamard.astype(jnp.bfloat16), (1, local_a))
+    signs = jnp.repeat(sylvester(local_a).astype(jnp.bfloat16), HB, axis=1)
+    table = jnp.concatenate(
+        [
+            jnp.pad(small, ((0, half - HB), (0, units))),
+            jnp.pad(signs, ((0, half - local_a), (units, 0))),
+        ],
+        axis=0,
+    )
+    pieces = depth // (LANES * ROWS)
+    out_pieces = width // (LANES * ROWS)
+    owners = units // LANES
+    chunk_rows = CHUNK_GROUPS * LANES
+    down_cols = 8 * LANES
+    bf16, f32 = jnp.bfloat16, jnp.float32
+    dma = pltpu.SemaphoreType.DMA
+    out = pl.pallas_call(
+        functools.partial(kernel, n),
+        out_shape=jax.ShapeDtypeStruct((width // LANES, LANES), bf16),
+        in_specs=[pl.BlockSpec(memory_space=pl.ANY)] * 9,
+        out_specs=pl.BlockSpec(memory_space=pltpu.VMEM),
+        scratch_shapes=[
+            pltpu.VMEM((SLOTS, 2, chunk_rows, units), bf16),
+            pltpu.VMEM(gate_scales.shape, f32),
+            pltpu.VMEM(up_scales.shape, f32),
+            pltpu.VMEM((width // down_cols, units, down_cols), bf16),
+            pltpu.VMEM((width // LANES, LANES), f32),
+            pltpu.VMEM((units, LANES), bf16),
+            pltpu.VMEM((LANES, 2 * units), bf16),
+            pltpu.VMEM((units, units), bf16),
+            pltpu.VMEM((pieces, n, ROWS, LANES), bf16),
+            pltpu.VMEM((n * ROWS, LANES), f32),
+            pltpu.VMEM((ROWS // 2, 2 * n, 2 * LANES), bf16),
+            pltpu.VMEM((2, n, units), f32),
+            pltpu.VMEM((owners, n, LANES), bf16),
+            pltpu.VMEM((n, n, LANES), bf16),
+            pltpu.VMEM((n, n, LANES), bf16),
+            pltpu.VMEM((owners, n, LANES), bf16),
+            pltpu.VMEM((n * ROWS, LANES), f32),
+            pltpu.VMEM((out_pieces, n, ROWS, LANES), bf16),
+            pltpu.VMEM((out_pieces, n, ROWS, LANES), bf16),
+            dma((SLOTS, 2)),
+            dma((5,)),
+            dma((width // down_cols,)),
+            dma((pieces,)),
+            dma((pieces, n - 1)),
+            dma((pieces, n)),
+            dma((owners,)),
+            dma((n,)),
+            dma((n - 1,)),
+            dma((owners,)),
+            dma((out_pieces, n - 1)),
+            dma((out_pieces, n)),
+        ],
+        compiler_params=pltpu.CompilerParams(
+            collective_id=0, has_side_effects=True, vmem_limit_bytes=67043328
+        ),
+    )(
+        tokens.reshape(depth // LANES, LANES), gate_codes, gate_scales, up_codes, up_scales, down_codes,
+        down_scales.reshape(width // LANES, LANES), spread, table,
+    )
+    return out.reshape(1, width)
+
+
+def fits(n, tokens, gate_codes, gate_scales, down_codes):
+    rows, depth = tokens.shape
+    units, width = down_codes.shape
+    return (
+        rows == 1
+        and n == ROWS
+        and HA % n == 0
+        and HA // n <= LANES // 2
+        and depth == gate_scales.shape[0] * LANES
+        and depth % (ROWS * LANES) == 0
+        and width % (ROWS * LANES) == 0
+        and units % LANES == 0
+        and units // LANES <= n
+    )
+
+
 def per_device(
     tokens, gate_codes, gate_scales, up_codes, up_scales, down_codes, down_scales, hadamard
 ):
+    n = lax.axis_size("hx")
+    if fits(n, tokens, gate_codes, gate_scales, down_codes):
+        return fused(
+            n, tokens, gate_codes, gate_scales, up_codes, up_scales, down_codes, down_scales, hadamard
+        )
     gate_weight = dequantize(gate_codes, gate_scales)
     up_weight = dequantize(up_codes, up_scales)
     tile_rows = lax.all_gather(tokens, "hx", axis=0, tiled=True)

time: 228 us -> 57.1 us (0.25)
  waiting for transfers between devices: 94.2 us -> 0 us
  Pallas kernels: 0 us -> 50 us
  other arithmetic: 42.7 us -> 4.18 us
  matrix products: 36.7 us -> 0 us
  blocking collectives: 34.2 us -> 0 us
  between operations: 13.6 us -> 0.03 us
  starting transfers between devices: 3.52 us -> 0 us
    unnamed x2 -> x0, waiting for transfers between devices: 87.5 us -> none
    pallas_call x0 -> x1, Pallas kernels: none -> 50 us  [fused(): pl.pallas_call(functools.partial(kernel, n), out_shape=jax.ShapeDtypeStru...]
    convert_element_type x3, other arithmetic: 40.8 us -> 2.48 us  [the longest x1 1.63 us: fused(): spread = ((lane[None, :] == (unit % HB)[:, None]) | (lane[None, :] == hal...]
    dot_general x5 -> x0, matrix products: 36.7 us -> none  [the longest x1 13.2 us: per_device(): jnp.dot(rotated, down_codes, preferred_element_type=jnp.float32)]
    all_gather x1 -> x0, blocking collectives: 24.8 us -> none  [per_device(): tile_rows = lax.all_gather(tokens, 'hx', axis=0, tiled=True)]
    all_to_all x1 -> x0, blocking collectives: 9.4 us -> none  [per_device(): lax.all_to_all(cube.reshape(row_count, FF).astype(jnp.bfloat16), 'hx', sp...]
    all_to_all x1 -> x0, waiting for transfers between devices: 6.69 us -> none  [per_device(): lax.all_to_all(hidden.astype(jnp.bfloat16), 'hx', split_axis=0, concat_ax...]
    all_to_all x1 -> x0, starting transfers between devices: 3.47 us -> none  [per_device(): lax.all_to_all(hidden.astype(jnp.bfloat16), 'hx', split_axis=0, concat_ax...]
  transfers between devices with their start and end apart: 2 -> 0, of which waited for: 2 -> 0; matrix products, arithmetic and copies ran while one was open for 0% -> 0% of each run, Pallas kernels for 0% -> 0%
where the time goes in v1:
time: 57.1 us; the launch traced here: 56.9 us
  Pallas kernels  50 us (88%)
  other arithmetic  4.18 us (7%)
  local copies, waits for them, and re-layouts  2.71 us (5%)
    pallas_call x1, Pallas kernels, fused(): pl.pallas_call(functools.partial(kernel, n), out_shape=jax.ShapeDtypeStru...  50 us
    convert_element_type x1, other arithmetic, fused(): spread = ((lane[None, :] == (unit % HB)[:, None]) | (lane[None, :] == hal...  1.63 us
    unnamed x3, local copies, waits for them, and re-layouts  1.36 us

profile of v1, /device:TPU:0, one launch (start us, length us, event | category | flops | bytes accessed | tf_op | source)
XLA Modules:
  0.0 56.9 jit_solution(3641578830113594068)
XLA Ops:
  0.0 0.0 copy-start
  0.0 0.1 fusion.9
  0.1 0.2 broadcast_in_dim.2
  0.3 0.4 reshape.110
  0.7 0.8 %convert_element_type.17 = bf16[52,52]{1,0:T(8,128)(2,1)S(1)} convert(s32[52,52]{1,0:T(8,128)} %param.15) | non-fusion elementwise | flops 2704 | bytes 16224 | tf_op jit(solution)/shard_map/convert_element_type | solution.py:276
  1.5 0.1 tile.4
  1.5 0.7 %tile.10 = bf16[52,1664]{1,0:T(8,128)(2,1)S(1)} reshape(bf16[52,32,52]{2,1,0:T(8,128)(2,1)S(1)} %tile.4) | data formatting | bytes 346112 | tf_op jit(solution)/shard_map/tile | solution.py:276
  2.2 1.0 %fusion.2.table_ref = bf16[128,3328]{1,0:T(8,128)(2,1)} fusion(bf16[32,1664]{1,0:T(8,128)(2,1)S(1)} %reshape.110, bf16[52,1664]{1,0:T(8,128)(2,1)S(1)} %tile.10), kind=kLoop, calls=%fused_computation.6 | loop fusion | flops 3407872 | bytes 1131520 | tf_op jit(solution)/shard_map/concatenate | solution.py:278
  3.2 1.6 %fusion.4.spread_ref = bf16[1664,128]{1,0:T(8,128)(2,1)} fusion(s32[1664]{0:T(1024)S(1)} %get-tuple-element.6, s32[1664]{0:T(1024)S(1)} %get-tuple-element.5), kind=kLoop, calls=%fused_computation.8 | loop fusion | flops 851968 | bytes 439296 | tf_op jit(solution)/shard_map/convert_element_type | solution.py:275
  4.9 0.0 copy-done
  4.9 0.7 %reduce = bf16[8192]{0:T(1024)(128)(2,1)} reduce(bf16[1,8192]{1,0:T(2,128)(2,1)S(1)} %copy-done, bf16[]{:T(256)} %constant.57), dimensions={0}, to_apply=%param.8.reduce_sub_computation | reduce | bytes 32770 | tf_op args[0]
  5.6 50.0 %shard_map.82 = bf16[64,128]{1,0:T(8,128)(2,1)} custom-call(bf16[64,128]{1,0:T(8,128)(2,1)} %bitcast.7, bf16[8192,1664]{1,0:T(8,128)(2,1)} %gate_ref.1, f32[64,1664]{1,0:T(8,128)} %gscale_ref.1, bf16[8192,1664]{1,0:T(8,128)(2,1)} %up_ref.1, f32[64,1664]{1,0:T(8,128)} %uscale_ref.1, bf16[1664,8192]{1,0:T(8,128)(2,1)} %down_ref.1, f32[64,128]{1,0:T(8,128)} %bitcast.9, ...), custom_call_target="tpu_custom_call" | custom-call | tf_op jit(solution)/shard_map/pallas_call | solution.py:292
  55.6 1.4 %copy.11 = bf16[1,1,64,128]{3,1,2,0:T(2,128)(2,1)} copy(bf16[1,1,64,128]{3,2,1,0:T(8,128)(2,1)} %bitcast.8) | data formatting | bytes 32768
  (4 shorter events, 0.0 us)
Async XLA Ops:
  0.0 4.9 %copy-start = (bf16[1,8192]{1,0:T(2,128)(2,1)S(1)}, bf16[1,8192]{1,0:T(2,128)(2,1)}, u32[]{:S(2)}) copy-start(bf16[1,8192]{1,0:T(2,128)(2,1)} %param.8) | copy-start | bytes 49156

commit v2 on v1

--- a/solution.py
+++ b/solution.py
@@ -37,10 +37,10 @@
 
 
 def kernel(
-    n, tok_ref, gate_ref, gscale_ref, up_ref, uscale_ref, down_ref, dscale_ref, spread_ref, table_ref,
+    n, tok_ref, gate_ref, gscale_ref, up_ref, uscale_ref, down_ref, dscale_ref, had_ref,
     out_ref,
-    ring, gs, us, down, ds, spread, table, local, tok, stage, lhs, acc, zbuf, recv_z, rbuf, rot, part, sendbuf, recv_c,
-    ring_sem, load_sem, down_sem, tok_own, tok_send, tok_recv, z_send, z_recv, r_send, r_recv, c_send, c_recv,
+    ring, gs, us, down, ds, had, corner, table, local, tok_row, tok_f32, tok_out_buf, tok, stage, lhs, acc, zbuf, recv_z, rbuf, rot, part, sendbuf, recv_c,
+    ring_sem, load_sem, down_sem, tok_send, tok_recv, z_send, z_recv, r_send, r_recv, c_send, c_recv,
 ):
     me = lax.axis_index("hx")
     pieces = tok.shape[0]
@@ -67,24 +67,25 @@
     loads = [
         pltpu.make_async_copy(src, dst, load_sem.at[i])
         for i, (src, dst) in enumerate(
-            ((spread_ref, spread), (table_ref, table), (gscale_ref, gs), (uscale_ref, us), (dscale_ref, ds))
-        )
-    ]
-    own_tok = [
-        pltpu.make_async_copy(tok_ref.at[pl.ds(p * ROWS, ROWS)], tok.at[p, me], tok_own.at[p])
-        for p in range(pieces)
+            ((tok_ref, tok_row), (had_ref, had), (dscale_ref, ds), (gscale_ref, gs), (uscale_ref, us))
+        )
     ]
 
     barrier = pltpu.get_barrier_semaphore()
     for peer in peers:
         pl.semaphore_signal(barrier, inc=1, device_id={"hx": peer}, device_id_type=pl.DeviceIdType.MESH)
-    for copy in own_tok:
-        copy.start()
     for copy in loads:
         copy.start()
     for c in range(SLOTS):
         gate_copy(c, c).start()
         up_copy(c, c).start()
+    loads[0].wait()
+    row = tok_row[...].astype(jnp.float32)
+    for k in range(pieces * ROWS):
+        tok_f32[k : k + 1, :] = row[:, k * LANES : (k + 1) * LANES]
+    tok_out_buf[...] = tok_f32[...].astype(jnp.bfloat16)
+    for p in range(pieces):
+        tok[p, me] = tok_out_buf[p * ROWS : (p + 1) * ROWS, :]
     pl.semaphore_wait(barrier, n - 1)
 
     def remote(src, dst, send_sem, recv_sem, peer):
@@ -95,12 +96,12 @@
 
     def tok_out(p, i):
         return remote(
-            tok_ref.at[pl.ds(p * ROWS, ROWS)], tok.at[p, me], tok_send.at[p, i], tok_recv.at[p, me], peers[i]
+            tok_out_buf.at[pl.ds(p * ROWS, ROWS)], tok.at[p, me], tok_send.at[p, i], tok_recv.at[p, me], peers[i]
         )
 
     def tok_in(p, i):
         return remote(
-            tok_ref.at[pl.ds(p * ROWS, ROWS)], tok.at[p, peers[i]], tok_send.at[p, i], tok_recv.at[p, peers[i]],
+            tok_out_buf.at[pl.ds(p * ROWS, ROWS)], tok.at[p, peers[i]], tok_send.at[p, i], tok_recv.at[p, peers[i]],
             peers[i],
         )
 
@@ -110,13 +111,49 @@
 
     lhs[...] = jnp.zeros_like(lhs)
     acc[...] = jnp.zeros_like(acc)
-    for copy in loads:
+    for copy in loads[1:]:
         copy.wait()
 
+    half = LANES // 2
+    hb = had.shape[0]
+    ha = units // hb
+    corner[...] = jnp.zeros_like(corner)
+    corner[:hb, :hb] = had[...].astype(jnp.float32)
+    left_bits = lax.broadcasted_iota(jnp.int32, (ha, ha), 0) & lax.broadcasted_iota(jnp.int32, (ha, ha), 1)
+    parity = jnp.zeros((ha, ha), jnp.int32)
+    for level in range(ha.bit_length() - 1):
+        parity = parity ^ (jnp.right_shift(left_bits, level) & 1)
+    corner[half : half + ha, half : half + ha] = (1 - 2 * parity).astype(jnp.float32)
+
+    def digits(unit):
+        high = jnp.floor((unit + 0.5) * (1.0 / hb))
+        return high, unit - hb * high
+
+    def wide(i, carry):
+        shape = (LANES, LANES)
+        unit = (lax.broadcasted_iota(jnp.int32, shape, 1) + i * LANES).astype(jnp.float32)
+        at = lax.broadcasted_iota(jnp.int32, shape, 0).astype(jnp.float32)
+        high, low = digits(unit)
+        pick = jnp.where((at == low) | (at == high + half), 1.0, 0.0).astype(jnp.bfloat16)
+        table[i] = jnp.dot(
+            corner[...].astype(jnp.bfloat16), pick, preferred_element_type=jnp.float32
+        ).astype(jnp.bfloat16)
+        return carry
+
+    lax.fori_loop(0, owners, wide, 0)
+    factors = jnp.concatenate([table[j] for j in range(owners)], axis=1)
+
     def build(i, carry):
+        shape = (LANES, LANES)
+        unit = (lax.broadcasted_iota(jnp.int32, shape, 0) + i * LANES).astype(jnp.float32)
+        at = lax.broadcasted_iota(jnp.int32, shape, 1).astype(jnp.float32)
+        high, low = digits(unit)
+        pick = jnp.concatenate(
+            [jnp.where(at == low, 1.0, 0.0), jnp.where(at == high + half, 1.0, 0.0)], axis=0
+        ).astype(jnp.bfloat16)
+        both = jnp.dot(pick, factors, preferred_element_type=jnp.float32)
         rows = pl.ds(pl.multiple_of(i * LANES, LANES), LANES)
-        both = jnp.dot(spread[rows, :], table[...], preferred_element_type=jnp.float32)
-        local[rows, :] = (both[:, :units] * both[:, units:]).astype(jnp.bfloat16)
+        local[rows, :] = (both[:LANES] * both[LANES:]).astype(jnp.bfloat16)
         return carry
 
     lax.fori_loop(0, units // LANES, build, 0)
@@ -125,7 +162,6 @@
     chunks_piece = chunks // pieces
     pairs_chunk = CHUNK_GROUPS // 2
     for p in range(pieces):
-        own_tok[p].wait()
         for i in range(n - 1):
             tok_in(p, i).wait_recv()
         stage[...] = tok[p].reshape(n * ROWS, LANES).astype(jnp.float32)
@@ -241,8 +277,9 @@
         total = recv_c[p, 0].astype(jnp.float32)
         for h in range(1, n):
             total = total + recv_c[p, h].astype(jnp.float32)
-        rows = slice(p * ROWS, (p + 1) * ROWS)
-        out_ref[rows, :] = (total * ds[rows, :]).astype(out_ref.dtype)
+        for r in range(ROWS):
+            cols = slice((p * ROWS + r) * LANES, (p * ROWS + r + 1) * LANES)
+            out_ref[:, cols] = (total[r : r + 1, :] * ds[:, cols]).astype(out_ref.dtype)
 
     for p in range(pieces):
         for i in range(n - 1):
@@ -266,22 +303,6 @@
 def fused(n, tokens, gate_codes, gate_scales, up_codes, up_scales, down_codes, down_scales, hadamard):
     depth, units = gate_codes.shape
     width = down_codes.shape[1]
-    local_a = HA // n
-    unit = jnp.arange(units, dtype=jnp.int32)
-    lane = jnp.arange(LANES, dtype=jnp.int32)
-    half = LANES // 2
-    spread = (
-        (lane[None, :] == (unit % HB)[:, None]) | (lane[None, :] == half + (unit // HB)[:, None])
-    ).astype(jnp.bfloat16)
-    small = jnp.tile(hadamard.astype(jnp.bfloat16), (1, local_a))
-    signs = jnp.repeat(sylvester(local_a).astype(jnp.bfloat16), HB, axis=1)
-    table = jnp.concatenate(
-        [
-            jnp.pad(small, ((0, half - HB), (0, units))),
-            jnp.pad(signs, ((0, half - local_a), (units, 0))),
-        ],
-        axis=0,
-    )
     pieces = depth // (LANES * ROWS)
     out_pieces = width // (LANES * ROWS)
     owners = units // LANES
@@ -291,18 +312,22 @@
     dma = pltpu.SemaphoreType.DMA
     out = pl.pallas_call(
         functools.partial(kernel, n),
-        out_shape=jax.ShapeDtypeStruct((width // LANES, LANES), bf16),
-        in_specs=[pl.BlockSpec(memory_space=pl.ANY)] * 9,
+        out_shape=jax.ShapeDtypeStruct((1, width), bf16),
+        in_specs=[pl.BlockSpec(memory_space=pl.ANY)] * 8,
         out_specs=pl.BlockSpec(memory_space=pltpu.VMEM),
         scratch_shapes=[
             pltpu.VMEM((SLOTS, 2, chunk_rows, units), bf16),
             pltpu.VMEM(gate_scales.shape, f32),
             pltpu.VMEM(up_scales.shape, f32),
             pltpu.VMEM((width // down_cols, units, down_cols), bf16),
-            pltpu.VMEM((width // LANES, LANES), f32),
-            pltpu.VMEM((units, LANES), bf16),
-            pltpu.VMEM((LANES, 2 * units), bf16),
+            pltpu.VMEM((1, width), f32),
+            pltpu.VMEM(hadamard.shape, hadamard.dtype),
+            pltpu.VMEM((LANES, LANES), f32),
+            pltpu.VMEM((owners, LANES, LANES), bf16),
             pltpu.VMEM((units, units), bf16),
+            pltpu.VMEM((1, depth), bf16),
+            pltpu.VMEM((depth // LANES, LANES), f32),
+            pltpu.VMEM((depth // LANES, LANES), bf16),
             pltpu.VMEM((pieces, n, ROWS, LANES), bf16),
             pltpu.VMEM((n * ROWS, LANES), f32),
             pltpu.VMEM((ROWS // 2, 2 * n, 2 * LANES), bf16),
@@ -317,7 +342,6 @@
             dma((SLOTS, 2)),
             dma((5,)),
             dma((width // down_cols,)),
-            dma((pieces,)),
             dma((pieces, n - 1)),
             dma((pieces, n)),
             dma((owners,)),
@@ -331,10 +355,9 @@
             collective_id=0, has_side_effects=True, vmem_limit_bytes=67043328
         ),
     )(
-        tokens.reshape(depth // LANES, LANES), gate_codes, gate_scales, up_codes, up_scales, down_codes,
-        down_scales.reshape(width // LANES, LANES), spread, table,
+        tokens, gate_codes, gate_scales, up_codes, up_scales, down_codes, down_scales.reshape(1, width), hadamard,
     )
-    return out.reshape(1, width)
+    return out
 
 
 def fits(n, tokens, gate_codes, gate_scales, down_codes):
@@ -345,6 +368,7 @@
         and n == ROWS
         and HA % n == 0
         and HA // n <= LANES // 2
+        and HB <= LANES // 2
         and depth == gate_scales.shape[0] * LANES
         and depth % (ROWS * LANES) == 0
         and width % (ROWS * LANES) == 0

time: 57.1 us -> 53.4 us (0.935)
  other arithmetic: 4.18 us -> 0 us
  Pallas kernels: 50 us -> 51.8 us
  local copies, waits for them, and re-layouts: 2.71 us -> 1.41 us
    convert_element_type x3 -> x0, other arithmetic: 2.48 us -> none  [the longest x1 1.63 us: fused(): spread = ((lane[None, :] == (unit % HB)[:, None]) | (lane[None, :] == hal...]
    pallas_call x1, Pallas kernels: 50 us -> 51.8 us  [fused(): pl.pallas_call(functools.partial(kernel, n), out_shape=jax.ShapeDtypeStru...]
    concatenate x1 -> x0, other arithmetic: 0.98 us -> none  [fused(): jnp.concatenate([jnp.pad(small, ((0, half - HB), (0, units))), jnp.pad(si...]
    another operation x2 -> x0, local copies, waits for them, and re-layouts: 0.79 us -> none  [fused(): small = jnp.tile(hadamard.astype(jnp.bfloat16), (1, local_a))]
    unnamed x1 -> x0, other arithmetic: 0.69 us -> none
    unnamed x3 -> x1, local copies, waits for them, and re-layouts: 1.36 us -> 1.41 us
where the time goes in v2:
time: 53.4 us; the launch traced here: 53.2 us
  Pallas kernels  51.8 us (97%)
  local copies, waits for them, and re-layouts  1.41 us (3%)
    pallas_call x1, Pallas kernels, fused(): pl.pallas_call(functools.partial(kernel, n), out_shape=jax.ShapeDtypeStru...  51.8 us
    unnamed x1, local copies, waits for them, and re-layouts  1.41 us

profile of v2, /device:TPU:0, one launch (start us, length us, event | category | flops | bytes accessed | tf_op | source)
XLA Modules:
  0.0 53.2 jit_solution(11568892313107243290)
XLA Ops:
  0.0 51.8 %shard_map.82 = bf16[1,8192]{1,0:T(2,128)(2,1)} custom-call(bf16[1,8192]{1,0:T(2,128)(2,1)} %tok_ref.1, bf16[8192,1664]{1,0:T(8,128)(2,1)} %gate_ref.1, f32[64,1664]{1,0:T(8,128)} %gscale_ref.1, bf16[8192,1664]{1,0:T(8,128)(2,1)} %up_ref.1, f32[64,1664]{1,0:T(8,128)} %uscale_ref.1, bf16[1664,8192]{1,0:T(8,128)(2,1)} %down_ref.1, f32[1,8192]{1,0:T(1,128)} %bitcast.1, ...), custom_call_target="tpu_custom_call" | custom-call | tf_op jit(solution)/shard_map/pallas_call | solution.py:313
  51.8 1.4 %copy.10 = bf16[1,8192]{1,0:T(2,128)(2,1)} copy(bf16[1,8192]{1,0:T(2,128)(2,1)} %shard_map.82) | data formatting | bytes 32768

commit v3 on v2

v3 whole, which is shorter than its diff:
```python
import functools
import math

import jax
import jax.numpy as jnp
from jax import lax
from jax.experimental import pallas as pl
from jax.experimental.pallas import tpu as pltpu
from jax.sharding import PartitionSpec as P

HA = 512
HB = 52
FF = 26624


def sylvester(size):
    index_vec = jnp.arange(size, dtype=jnp.int32)
    parity = jnp.zeros((size, size), jnp.int32)
    for level in range(max(size.bit_length() - 1, 0)):
        left_bits = jnp.right_shift(index_vec[:, None], level) & 1
        right_bits = jnp.right_shift(index_vec[None, :], level) & 1
        parity = parity + left_bits * right_bits
    return (1 - 2 * (parity % 2)).astype(jnp.float32)


def dequantize(codes, scales):
    row_total, col_total = codes.shape
    group_total = scales.shape[0]
    grouped = codes.astype(jnp.float32).reshape(group_total, row_total // group_total, col_total)
    return (grouped * scales[:, None, :]).reshape(row_total, col_total).astype(jnp.bfloat16)


LANES = 128
ROWS = 16
CHUNK_GROUPS = 4


def kernel(
    n, parts, tok_ref, gate_ref, gscale_ref, up_ref, uscale_ref, down_ref, dscale_ref, had_ref,
    out_ref,
    ring, gs, us, down, ds, had, corner, table, local, tok_row, tok_f32, tok_out_buf, tok, stage, lhs, acc, zbuf, recv_z, rbuf, rot, part, sendbuf, recv_c, swap_out, swap_in,
    ring_sem, load_sem, down_sem, tok_send, tok_recv, z_send, z_recv, r_send, r_recv, c_send, c_recv, swap_send, swap_recv,
):
    me = lax.axis_index("hx")
    pieces = tok.shape[0]
    units = gate_ref.shape[1]
    owners = units // LANES
    chunk_rows = ring.shape[2]
    chunks = ring.shape[0]
    mine = lax.axis_index("groups")
    me_all = mine * n + me
    total_n = parts * n
    half_groups = gs.shape[0]
    down_chunks, _, down_cols = down.shape
    out_pieces = recv_c.shape[0]
    peers = [lax.rem(me + step, n) for step in range(1, n)]
    everyone = [lax.rem(me_all + step, total_n) for step in range(1, total_n)]
    sides = [lax.div(peer, n) for peer in everyone]
    spots = [lax.rem(peer, n) for peer in everyone]

    def gate_copy(c, slot):
        rows = pl.ds(pl.multiple_of((mine * chunks + c) * chunk_rows, chunk_rows), chunk_rows)
        return pltpu.make_async_copy(gate_ref.at[rows], ring.at[slot, 0], ring_sem.at[slot, 0])

    def up_copy(c, slot):
        rows = pl.ds(pl.multiple_of((mine * chunks + c) * chunk_rows, chunk_rows), chunk_rows)
        return pltpu.make_async_copy(up_ref.at[rows], ring.at[slot, 1], ring_sem.at[slot, 1])

    def down_copy(c):
        cols = pl.ds(pl.multiple_of((mine * down_chunks + c) * down_cols, down_cols), down_cols)
        return pltpu.make_async_copy(down_ref.at[:, cols], down.at[c], down_sem.at[c])

    loads = [
        pltpu.make_async_copy(src, dst, load_sem.at[i])
        for i, (src, dst) in enumerate(
            (
                (tok_ref, tok_row),
                (had_ref, had),
                (dscale_ref, ds),
                (gscale_ref.at[pl.ds(pl.multiple_of(mine * half_groups, 8), half_groups)], gs),
                (uscale_ref.at[pl.ds(pl.multiple_of(mine * half_groups, 8), half_groups)], us),
            )
        )
    ]

    barrier = pltpu.get_barrier_semaphore()
    for side, spot in zip(sides, spots):
        pl.semaphore_signal(
            barrier, inc=1, device_id={"groups": side, "hx": spot}, device_id_type=pl.DeviceIdType.MESH
        )
    for copy in loads:
        copy.start()
    for c in range(chunks):
        gate_copy(c, c).start()
        up_copy(c, c).start()
    for c in range(down_chunks):
        down_copy(c).start()
    loads[0].wait()
    row = tok_row[...].astype(jnp.float32)
    for k in range(parts * pieces * ROWS):
        tok_f32[k : k + 1, :] = row[:, k * LANES : (k + 1) * LANES]
    tok_out_buf[...] = tok_f32[...].astype(jnp.bfloat16)
    for p in range(pieces):
        tok[p, me_all] = tok_out_buf[pl.ds(pl.multiple_of((mine * pieces + p) * ROWS, ROWS), ROWS), :]
    pl.semaphore_wait(barrier, total_n - 1)

    def remote(src, dst, send_sem, recv_sem, peer, side=None):
        side = mine if side is None else side
        return pltpu.make_async_remote_copy(
            src_ref=src, dst_ref=dst, send_sem=send_sem, recv_sem=recv_sem,
            device_id={"groups": side, "hx": peer}, device_id_type=pl.DeviceIdType.MESH,
        )

    def tok_copy(p, i, slot):
        rows = pl.ds(pl.multiple_of((sides[i] * pieces + p) * ROWS, ROWS), ROWS)
        return remote(
            tok_out_buf.at[rows], tok.at[p, slot], tok_send.at[p, i], tok_recv.at[p, slot], spots[i], sides[i]
        )

    for p in range(pieces):
        for i in range(total_n - 1):
            tok_copy(p, i, me_all).start()

    lhs[...] = jnp.zeros_like(lhs)
    acc[...] = jnp.zeros_like(acc)
    for copy in loads[1:]:
        copy.wait()

    half = LANES // 2
    hb = had.shape[0]
    ha = units // hb
    corner[...] = jnp.zeros_like(corner)
    corner[:hb, :hb] = had[...].astype(jnp.float32)
    left_bits = lax.broadcasted_iota(jnp.int32, (ha, ha), 0) & lax.broadcasted_iota(jnp.int32, (ha, ha), 1)
    parity = jnp.zeros((ha, ha), jnp.int32)
    for level in range(ha.bit_length() - 1):
        parity = parity ^ (jnp.right_shift(left_bits, level) & 1)
    corner[half : half + ha, half : half + ha] = (1 - 2 * parity).astype(jnp.float32)

    def digits(unit):
        high = jnp.floor((unit + 0.5) * (1.0 / hb))
        return high, unit - hb * high

    def wide(i, carry):
        shape = (LANES, LANES)
        unit = (lax.broadcasted_iota(jnp.int32, shape, 1) + i * LANES).astype(jnp.float32)
        at = lax.broadcasted_iota(jnp.int32, shape, 0).astype(jnp.float32)
        high, low = digits(unit)
        pick = jnp.where((at == low) | (at == high + half), 1.0, 0.0).astype(jnp.bfloat16)
        table[i] = jnp.dot(
            corner[...].astype(jnp.bfloat16), pick, preferred_element_type=jnp.float32
        ).astype(jnp.bfloat16)
        return carry

    lax.fori_loop(0, owners, wide, 0)
    factors = jnp.concatenate([table[j] for j in range(owners)], axis=1)

    def build(i, carry):
        shape = (LANES, LANES)
        unit = (lax.broadcasted_iota(jnp.int32, shape, 0) + i * LANES).astype(jnp.float32)
        at = lax.broadcasted_iota(jnp.int32, shape, 1).astype(jnp.float32)
        high, low = digits(unit)
        pick = jnp.concatenate(
            [jnp.where(at == low, 1.0, 0.0), jnp.where(at == high + half, 1.0, 0.0)], axis=0
        ).astype(jnp.bfloat16)
        both = jnp.dot(pick, factors, preferred_element_type=jnp.float32)
        rows = pl.ds(pl.multiple_of(i * LANES, LANES), LANES)
        local[rows, :] = (both[:LANES] * both[LANES:]).astype(jnp.bfloat16)
        return carry

    lax.fori_loop(0, units // LANES, build, 0)

    pairs_piece = ROWS // 2
    chunks_piece = chunks // pieces
    pairs_chunk = CHUNK_GROUPS // 2
    for p in range(pieces):
        for i in range(total_n - 1):
            tok_copy(p, i, everyone[i]).wait_recv()
        stage[...] = tok[p].reshape(total_n * ROWS, LANES).astype(jnp.float32)
        for q in range(pairs_piece):
            lhs[q, :total_n, :LANES] = stage[pl.ds(2 * q, total_n, stride=ROWS), :].astype(jnp.bfloat16)
            lhs[q, total_n:, LANES:] = stage[pl.ds(2 * q + 1, total_n, stride=ROWS), :].astype(jnp.bfloat16)

        def step(k, carry):
            c = p * chunks_piece + k
            slot = c
            gate_copy(c, slot).wait()
            up_copy(c, slot).wait()
            for q in range(pairs_chunk):
                left = lhs[k * pairs_chunk + q]
                row = c * CHUNK_GROUPS + 2 * q
                for w, scale in ((0, gs), (1, us)):
                    res = jnp.dot(
                        left, ring[slot, w, 2 * q * LANES : 2 * (q + 1) * LANES, :],
                        preferred_element_type=jnp.float32,
                    )
                    acc[w] += res[:total_n] * scale[pl.ds(row, 1), :] + res[total_n:] * scale[pl.ds(row + 1, 1), :]

            return carry

        lax.fori_loop(0, chunks_piece, step, 0)
    theirs = parts - 1 - mine
    for w in range(2):
        swap_out[w] = acc[w, pl.ds(pl.multiple_of(theirs * n, n), n), :].astype(jnp.bfloat16)
    swap = remote(swap_out, swap_in, swap_send, swap_recv, me, theirs)
    swap.start()
    own = pl.ds(pl.multiple_of(mine * n, n), n)
    swap.wait_recv()
    gate = acc[0, own, :] + swap_in[0].astype(jnp.float32)
    up_part = acc[1, own, :] + swap_in[1].astype(jnp.float32)
    hidden = (gate / (1.0 + jnp.exp(-gate)) * up_part).astype(jnp.bfloat16)
    turned = jnp.dot(hidden, local[...], preferred_element_type=jnp.float32).astype(jnp.bfloat16)
    for j in range(owners):
        zbuf[j] = turned[:, j * LANES : (j + 1) * LANES]

    def z_out(j):
        return remote(zbuf.at[j], recv_z.at[me], z_send.at[j], z_recv.at[me], j)

    for j in range(owners):

        @pl.when(me != j)
        def _():
            z_out(j).start()

        @pl.when(me == j)
        def _():
            recv_z[j] = zbuf[j]

    def r_out(i):
        return remote(
            rbuf.at[spots[i]], rot.at[mine, me], r_send.at[i], r_recv.at[mine, me], spots[i], sides[i]
        )

    @pl.when(me < owners)
    def _():
        for i in range(n - 1):
            remote(zbuf.at[0], recv_z.at[peers[i]], z_send.at[0], z_recv.at[peers[i]], peers[i]).wait_recv()
        cube = [recv_z[h].astype(jnp.float32) for h in range(n)]
        span = 1
        while span < n:
            nxt = list(cube)
            for h in range(n):
                if h & span == 0:
                    nxt[h] = cube[h] + cube[h | span]
                    nxt[h | span] = cube[h] - cube[h | span]
            cube = nxt
            span *= 2
        for h in range(n):
            rbuf[h] = (cube[h] * (1.0 / math.sqrt(FF))).astype(jnp.bfloat16)
        for i in range(total_n - 1):
            r_out(i).start()
        rot[mine, me] = rbuf[me]

    for j in range(owners):
        for side in range(parts):

            @pl.when(jnp.logical_or(me != j, mine != side))
            def _():
                remote(rbuf.at[0], rot.at[side, j], r_send.at[0], r_recv.at[side, j], j, theirs).wait_recv()

    rotated = jnp.concatenate(
        [jnp.concatenate([rot[side, j] for j in range(owners)], axis=1) for side in range(parts)], axis=0
    )

    def c_copy(p, i, slot):
        return remote(
            sendbuf.at[p, everyone[i]], recv_c.at[p, slot], c_send.at[p, i], c_recv.at[p, slot], spots[i], sides[i]
        )

    per_piece = down_chunks // out_pieces
    blocks = down_cols // LANES
    for p in range(out_pieces):
        for k in range(per_piece):
            c = p * per_piece + k
            down_copy(c).wait()
            res = jnp.dot(rotated, down[c], preferred_element_type=jnp.float32)
            for b in range(blocks):
                part[pl.ds(k * blocks + b, total_n, stride=ROWS), :] = res[:, b * LANES : (b + 1) * LANES]
        sendbuf[p] = part[...].astype(jnp.bfloat16).reshape(total_n, ROWS, LANES)
        for i in range(total_n - 1):
            c_copy(p, i, me_all).start()
        recv_c[p, me_all] = sendbuf[p, me_all]

    for p in range(out_pieces):
        for i in range(total_n - 1):
            c_copy(p, i, everyone[i]).wait_recv()
        for side in range(parts):
            total = recv_c[p, side * n].astype(jnp.float32)
            for h in range(1, n):
                total = total + recv_c[p, side * n + h].astype(jnp.float32)
            for r in range(ROWS):
                at = ((side * out_pieces + p) * ROWS + r) * LANES
                cols = slice(at, at + LANES)
                out_ref[:, cols] = (total[r : r + 1, :] * ds[:, cols]).astype(out_ref.dtype)

    swap.wait_send()
    for p in range(pieces):
        for i in range(total_n - 1):
            tok_copy(p, i, me_all).wait_send()
    for j in range(owners):

        @pl.when(me != j)
        def _():
            z_out(j).wait_send()

    @pl.when(me < owners)
    def _():
        for i in range(total_n - 1):
            r_out(i).wait_send()

    for p in range(out_pieces):
        for i in range(total_n - 1):
            c_copy(p, i, me_all).wait_send()


def fused(n, parts, tokens, gate_codes, gate_scales, up_codes, up_scales, down_codes, down_scales, hadamard):
    depth, units = gate_codes.shape
    width = down_codes.shape[1]
    pieces = depth // (LANES * ROWS * parts)
    out_pieces = width // (LANES * ROWS * parts)
    total_n = parts * n
    owners = units // LANES
    chunk_rows = CHUNK_GROUPS * LANES
    down_cols = 8 * LANES
    bf16, f32 = jnp.bfloat16, jnp.float32
    dma = pltpu.SemaphoreType.DMA
    out = pl.pallas_call(
        functools.partial(kernel, n, parts),
        out_shape=jax.ShapeDtypeStruct((1, width), bf16),
        in_specs=[pl.BlockSpec(memory_space=pl.ANY)] * 8,
        out_specs=pl.BlockSpec(memory_space=pltpu.VMEM),
        scratch_shapes=[
            pltpu.VMEM((depth // parts // chunk_rows, 2, chunk_rows, units), bf16),
            pltpu.VMEM((gate_scales.shape[0] // parts, units), f32),
            pltpu.VMEM((up_scales.shape[0] // parts, units), f32),
            pltpu.VMEM((width // parts // down_cols, units, down_cols), bf16),
            pltpu.VMEM((1, width), f32),
            pltpu.VMEM(hadamard.shape, hadamard.dtype),
            pltpu.VMEM((LANES, LANES), f32),
            pltpu.VMEM((owners, LANES, LANES), bf16),
            pltpu.VMEM((units, units), bf16),
            pltpu.VMEM((1, depth), bf16),
            pltpu.VMEM((depth // LANES, LANES), f32),
            pltpu.VMEM((depth // LANES, LANES), bf16),
            pltpu.VMEM((pieces, total_n, ROWS, LANES), bf16),
            pltpu.VMEM((total_n * ROWS, LANES), f32),
            pltpu.VMEM((ROWS // 2, 2 * total_n, 2 * LANES), bf16),
            pltpu.VMEM((2, total_n, units), f32),
            pltpu.VMEM((owners, n, LANES), bf16),
            pltpu.VMEM((n, n, LANES), bf16),
            pltpu.VMEM((n, n, LANES), bf16),
            pltpu.VMEM((parts, owners, n, LANES), bf16),
            pltpu.VMEM((total_n * ROWS, LANES), f32),
            pltpu.VMEM((out_pieces, total_n, ROWS, LANES), bf16),
            pltpu.VMEM((out_pieces, total_n, ROWS, LANES), bf16),
            pltpu.VMEM((2, n, units), bf16),
            pltpu.VMEM((2, n, units), bf16),
            dma((depth // parts // chunk_rows, 2)),
            dma((5,)),
            dma((width // parts // down_cols,)),
            dma((pieces, total_n - 1)),
            dma((pieces, total_n)),
            dma((owners,)),
            dma((n,)),
            dma((total_n - 1,)),
            dma((parts, owners)),
            dma((out_pieces, total_n - 1)),
            dma((out_pieces, total_n)),
            dma,
            dma,
        ],
        compiler_params=pltpu.CompilerParams(
            collective_id=0, has_side_effects=True, vmem_limit_bytes=67043328
        ),
    )(
        tokens, gate_codes, gate_scales, up_codes, up_scales, down_codes, down_scales.reshape(1, width), hadamard,
    )
    return out


def fits(n, parts, tokens, gate_codes, gate_scales, down_codes):
    rows, depth = tokens.shape
    units, width = down_codes.shape
    return (
        rows == 1
        and parts == 2
        and n == ROWS
        and HA % n == 0
        and HA // n <= LANES // 2
        and HB <= LANES // 2
        and depth == gate_scales.shape[0] * LANES
        and depth % (ROWS * LANES * parts) == 0
        and width % (ROWS * LANES * parts) == 0
        and units % LANES == 0
        and units // LANES <= n
    )


def per_device(
    tokens, gate_codes, gate_scales, up_codes, up_scales, down_codes, down_scales, hadamard
):
    n = lax.axis_size("hx")
    parts = lax.axis_size("groups")
    if fits(n, parts, tokens, gate_codes, gate_scales, down_codes):
        return fused(
            n, parts, tokens, gate_codes, gate_scales, up_codes, up_scales, down_codes, down_scales, hadamard
        )
    gate_weight = dequantize(gate_codes, gate_scales)
    up_weight = dequantize(up_codes, up_scales)
    tile_rows = lax.all_gather(tokens, "hx", axis=0, tiled=True)
    gate = jnp.dot(tile_rows, gate_weight, preferred_element_type=jnp.float32)
    up_part = jnp.dot(tile_rows, up_weight, preferred_element_type=jnp.float32)
    hidden = jax.nn.silu(gate) * up_part
    factor = hadamard.astype(jnp.float32)
    gathered = lax.all_to_all(
        hidden.astype(jnp.bfloat16), "hx", split_axis=0, concat_axis=1, tiled=True
    ).astype(hidden.dtype)
    row_count = gathered.shape[0]
    cube = gathered.reshape(row_count, HA, HB)
    cube = jnp.einsum("tab,ac->tcb", cube, sylvester(HA), precision=lax.Precision.HIGHEST)
    cube = jnp.einsum("tcb,bd->tcd", cube, factor, precision=lax.Precision.HIGHEST)
    turned = lax.all_to_all(
        cube.reshape(row_count, FF).astype(jnp.bfloat16),
        "hx",
        split_axis=1,
        concat_axis=0,
        tiled=True,
    ).astype(jnp.float32)
    rotated = (turned * (1.0 / math.sqrt(FF))).astype(jnp.bfloat16)
    summed = lax.psum_scatter(
        jnp.dot(rotated, down_codes, preferred_element_type=jnp.float32),
        "hx",
        scatter_dimension=0,
        tiled=True,
    )
    mixed = (summed * down_scales[None, :]).astype(jnp.bfloat16)
    return mixed


def solution(mesh):
    in_specs = (
        P(("groups", "hx"), None),
        P(None, "hx"),
        P(None, "hx"),
        P(None, "hx"),
        P(None, "hx"),
        P("hx", None),
        P(),
        P(),
    )
    out_specs = P(("groups", "hx"), None)
    return jax.shard_map(
        per_device, mesh=mesh, in_specs=in_specs, out_specs=out_specs, check_vma=False
    )
```

time: 53.4 us -> 57.3 us (1.073)
  Pallas kernels: 51.8 us -> 55.8 us
    pallas_call x1, Pallas kernels: 51.8 us -> 55.8 us  [fused(): pl.pallas_call(functools.partial(kernel, n, parts), out_shape=jax.ShapeDt...]
where the time goes in v3:
time: 57.3 us; the launch traced here: 57.2 us
  Pallas kernels  55.8 us (97%)
  local copies, waits for them, and re-layouts  1.41 us (2%)
    pallas_call x1, Pallas kernels, fused(): pl.pallas_call(functools.partial(kernel, n, parts), out_shape=jax.ShapeDt...  55.8 us
    unnamed x1, local copies, waits for them, and re-layouts  1.41 us

profile of v3, /device:TPU:0, one launch (start us, length us, event | category | flops | bytes accessed | tf_op | source)
XLA Modules:
  0.0 57.2 jit_solution(9073807804728787255)
XLA Ops:
  0.0 55.8 %shard_map.82 = bf16[1,8192]{1,0:T(2,128)(2,1)} custom-call(bf16[1,8192]{1,0:T(2,128)(2,1)} %tok_ref.1, bf16[8192,1664]{1,0:T(8,128)(2,1)} %gate_ref.1, f32[64,1664]{1,0:T(8,128)} %gscale_ref.1, bf16[8192,1664]{1,0:T(8,128)(2,1)} %up_ref.1, f32[64,1664]{1,0:T(8,128)} %uscale_ref.1, bf16[1664,8192]{1,0:T(8,128)(2,1)} %down_ref.1, f32[1,8192]{1,0:T(1,128)} %bitcast.1, ...), custom_call_target="tpu_custom_call" | custom-call | tf_op jit(solution)/shard_map/pallas_call | solution.py:327
  55.8 1.4 %copy.10 = bf16[1,8192]{1,0:T(2,128)(2,1)} copy(bf16[1,8192]{1,0:T(2,128)(2,1)} %shard_map.82) | data formatting | bytes 32768

commit v4 on v2

--- a/solution.py
+++ b/solution.py
@@ -86,33 +86,7 @@
     tok_out_buf[...] = tok_f32[...].astype(jnp.bfloat16)
     for p in range(pieces):
         tok[p, me] = tok_out_buf[p * ROWS : (p + 1) * ROWS, :]
-    pl.semaphore_wait(barrier, n - 1)
-
-    def remote(src, dst, send_sem, recv_sem, peer):
-        return pltpu.make_async_remote_copy(
-            src_ref=src, dst_ref=dst, send_sem=send_sem, recv_sem=recv_sem,
-            device_id={"hx": peer}, device_id_type=pl.DeviceIdType.MESH,
-        )
-
-    def tok_out(p, i):
-        return remote(
-            tok_out_buf.at[pl.ds(p * ROWS, ROWS)], tok.at[p, me], tok_send.at[p, i], tok_recv.at[p, me], peers[i]
-        )
-
-    def tok_in(p, i):
-        return remote(
-            tok_out_buf.at[pl.ds(p * ROWS, ROWS)], tok.at[p, peers[i]], tok_send.at[p, i], tok_recv.at[p, peers[i]],
-            peers[i],
-        )
-
-    for p in range(pieces):
-        for i in range(n - 1):
-            tok_out(p, i).start()
-
-    lhs[...] = jnp.zeros_like(lhs)
-    acc[...] = jnp.zeros_like(acc)
-    for copy in loads[1:]:
-        copy.wait()
+    loads[1].wait()
 
     half = LANES // 2
     hb = had.shape[0]
@@ -156,7 +130,36 @@
         local[rows, :] = (both[:LANES] * both[LANES:]).astype(jnp.bfloat16)
         return carry
 
-    lax.fori_loop(0, units // LANES, build, 0)
+    lax.fori_loop(0, owners // 2, build, 0)
+
+    pl.semaphore_wait(barrier, n - 1)
+
+    def remote(src, dst, send_sem, recv_sem, peer):
+        return pltpu.make_async_remote_copy(
+            src_ref=src, dst_ref=dst, send_sem=send_sem, recv_sem=recv_sem,
+            device_id={"hx": peer}, device_id_type=pl.DeviceIdType.MESH,
+        )
+
+    def tok_out(p, i):
+        return remote(
+            tok_out_buf.at[pl.ds(p * ROWS, ROWS)], tok.at[p, me], tok_send.at[p, i], tok_recv.at[p, me], peers[i]
+        )
+
+    def tok_in(p, i):
+        return remote(
+            tok_out_buf.at[pl.ds(p * ROWS, ROWS)], tok.at[p, peers[i]], tok_send.at[p, i], tok_recv.at[p, peers[i]],
+            peers[i],
+        )
+
+    for p in range(pieces):
+        for i in range(n - 1):
+            tok_out(p, i).start()
+
+    lhs[...] = jnp.zeros_like(lhs)
+    acc[...] = jnp.zeros_like(acc)
+    lax.fori_loop(owners // 2, owners, build, 0)
+    for copy in loads[2:]:
+        copy.wait()
 
     pairs_piece = ROWS // 2
     chunks_piece = chunks // pieces

time: 53.4 us -> 52.7 us (0.987)
  Pallas kernels: 51.8 us -> 51.1 us
    pallas_call x1, Pallas kernels: 51.8 us -> 51.1 us  [fused(): pl.pallas_call(functools.partial(kernel, n), out_shape=jax.ShapeDtypeStru...]
where the time goes in v4:
time: 52.7 us; the launch traced here: 52.5 us
  Pallas kernels  51.1 us (97%)
  local copies, waits for them, and re-layouts  1.41 us (3%)
    pallas_call x1, Pallas kernels, fused(): pl.pallas_call(functools.partial(kernel, n), out_shape=jax.ShapeDtypeStru...  51.1 us
    unnamed x1, local copies, waits for them, and re-layouts  1.41 us

profile of v4, /device:TPU:0, one launch (start us, length us, event | category | flops | bytes accessed | tf_op | source)
XLA Modules:
  0.0 52.5 jit_solution(16595079276208118687)
XLA Ops:
  0.0 51.1 %shard_map.82 = bf16[1,8192]{1,0:T(2,128)(2,1)} custom-call(bf16[1,8192]{1,0:T(2,128)(2,1)} %tok_ref.1, bf16[8192,1664]{1,0:T(8,128)(2,1)} %gate_ref.1, f32[64,1664]{1,0:T(8,128)} %gscale_ref.1, bf16[8192,1664]{1,0:T(8,128)(2,1)} %up_ref.1, f32[64,1664]{1,0:T(8,128)} %uscale_ref.1, bf16[1664,8192]{1,0:T(8,128)(2,1)} %down_ref.1, f32[1,8192]{1,0:T(1,128)} %bitcast.1, ...), custom_call_target="tpu_custom_call" | custom-call | tf_op jit(solution)/shard_map/pallas_call | solution.py:316
  51.1 1.4 %copy.10 = bf16[1,8192]{1,0:T(2,128)(2,1)} copy(bf16[1,8192]{1,0:T(2,128)(2,1)} %shard_map.82) | data formatting | bytes 32768
